TPU v7x, 128 devices: a whole 4x4x4 slice. The times are simulated.
128 devices in a mesh: dx: 8 (over y_lo, x), dy: 16 (over y_hi, z, core).
Axes of the slice: x: 4, y: 4 (y_hi: 2, y_lo: 2; y = y_hi * 2 + y_lo), z: 4, core: 2. Of those that a mesh axis runs over, the one named last changes fastest.
Arguments:
- fine_nodes: bfloat16 [256, 256, 512], P('dx', 'dy'), may hold values from -6 to 6
- fine_edges: bfloat16 [6, 256, 256, 512], P(None, 'dx', 'dy'), may hold values from -6 to 6
- fine_links: int32 [6, 256, 256], P(None, 'dx', 'dy'), may hold values from 0 to 48
- mid_nodes: bfloat16 [64, 64, 512], P('dx', 'dy'), may hold values from -6 to 6
- mid_edges: bfloat16 [6, 64, 64, 512], P(None, 'dx', 'dy'), may hold values from -6 to 6
- mid_links: int32 [6, 64, 64], P(None, 'dx', 'dy'), may hold values from 0 to 8
- coarse_nodes: bfloat16 [16, 16, 512], replicated, may hold values from -6 to 6
- coarse_edges: bfloat16 [6, 16, 16, 512], replicated, may hold values from -6 to 6
- coarse_links: int32 [6, 16, 16], replicated, may hold values from 0 to 255
- edge_self: bfloat16 [1, 512, 1536], replicated, may hold values from -0.25 to 0.25
- edge_sender: bfloat16 [1, 512, 1536], replicated, may hold values from -0.25 to 0.25
- edge_receiver: bfloat16 [1, 512, 1536], replicated, may hold values from -0.25 to 0.25
- edge_bias: float32 [1, 1536], replicated, may hold values from -6 to 6
- edge_output: bfloat16 [1, 1536, 512], replicated, may hold values from -0.15625 to 0.15625
- edge_gain: float32 [1, 512], replicated, may hold values from 0.1 to 1.9
- edge_shift: float32 [1, 512], replicated, may hold values from -3 to 3
- node_self: bfloat16 [1, 512, 1536], replicated, may hold values from -0.25 to 0.25
- node_summed: bfloat16 [1, 512, 1536], replicated, may hold values from -0.109375 to 0.109375
- node_bias: float32 [1, 1536], replicated, may hold values from -6 to 6
- node_output: bfloat16 [1, 1536, 512], replicated, may hold values from -0.15625 to 0.15625
- node_gain: float32 [1, 512], replicated, may hold values from 0.1 to 1.9
- node_shift: float32 [1, 512], replicated, may hold values from -3 to 3
- prolongation: bfloat16 [1, 512, 512], replicated, may hold values from -0.25 to 0.25
- pooling: bfloat16 [1, 512, 512], replicated, may hold values from -0.25 to 0.25
Outputs:
- fine_out: bfloat16 [256, 256, 512], P('dx', 'dy')
- fine_edges_out: bfloat16 [6, 256, 256, 512], P(None, 'dx', 'dy')
- mid_out: bfloat16 [64, 64, 512], P('dx', 'dy')
- mid_edges_out: bfloat16 [6, 64, 64, 512], P(None, 'dx', 'dy')
- coarse_out: bfloat16 [16, 16, 512], replicated
- coarse_edges_out: bfloat16 [6, 16, 16, 512], replicated
Inputs may be any that keep to these rules, and one draw needn't show every extreme that they name: `fine_links`: code q names the sender at offset (q // 7 - 3, q % 7 - 3) from the receiver. `mid_links`: code q names the sender at offset (q // 3 - 1, q % 3 - 1) from the receiver.
All inputs are finite; a program needn't handle non-finite values.
Results may differ from a plain program's by a relative error of at most 0.012.
Values may be sent and summed in bfloat16 or wider, within the bound.
No kernel may reach another device: no remote copies, remote signals or barrier semaphores. Data moves between devices by JAX's collectives and lax.ppermute only.
A program may use at most 128 MiB of HBM per device.

v0:
```python
import jax
import jax.numpy as jnp
from jax import lax
from jax.sharding import Mesh
from jax.sharding import PartitionSpec as P

FINE_REACH = 3
MID_REACH = 1
DX = ("dx_0", "dx_1")
DY = ("dy_0", "dy_1", "dy_2")
epsilon = 1e-05


def with_halo(value, sides, width):
    for axis, dim in sides:
        count, length = (lax.axis_size(axis), value.shape[dim])
        up = [(i, (i + 1) % count) for i in range(count)]
        down = [(j, i) for i, j in up]
        last = lax.slice_in_dim(value, length - width, length, axis=dim)
        leading = lax.slice_in_dim(value, 0, width, axis=dim)
        before = lax.ppermute(last, axis, up)
        after = lax.ppermute(leading, axis, down)
        value = jnp.concatenate([before, value, after], axis=dim)
    return value


def joined_along(blocks, dim):
    dims = list(blocks.shape[1:])
    dims[dim] *= blocks.shape[0]
    return jnp.moveaxis(blocks, 0, dim).reshape(dims)


def all_blocks(value, axes, turns):
    blocks = value[None]
    for k in turns:
        blocks = lax.all_gather(blocks, axes[k], axis=0, tiled=True)
    block = [lax.axis_size(axes[k]) for k in reversed(turns)]
    blocks = blocks.reshape(*block, *value.shape)
    turned = sorted(range(len(turns)), key=lambda place: turns[len(turns) - 1 - place])
    return blocks.transpose(*turned, *range(len(turns), blocks.ndim)).reshape(-1, *value.shape)


def gather_axes(value, axes, turns, dim):
    return joined_along(all_blocks(value, axes, turns), dim)


def normalize(values, gain_term, shift_term):
    average = jnp.mean(values, axis=-1, keepdims=True)
    centred = values - average
    variance = jnp.mean(centred * centred, axis=-1, keepdims=True)
    return centred * lax.rsqrt(variance + epsilon) * gain_term + shift_term


def level_update(nodes, edges, sender_terms, senders, weights):
    (
        self_matrix,
        receiver_matrix,
        edge_bias,
        edge_output,
        edge_gain,
        edge_shift,
        node_self,
        node_summed,
        node_bias,
        node_output,
        node_gain,
        node_shift,
    ) = weights
    fanout, height, breadth, feature = edges.shape
    places = height * breadth
    flat_nodes = nodes.reshape(places, feature)
    flat_edges = edges.reshape(fanout * places, feature)
    receiver = jnp.dot(flat_nodes, receiver_matrix, preferred_element_type=jnp.float32) + edge_bias
    latent = jnp.dot(flat_edges, self_matrix, preferred_element_type=jnp.float32).reshape(
        fanout, places, -1
    )
    latent = (
        latent + jnp.take(sender_terms, senders.reshape(fanout, places), axis=0) + receiver[None]
    )
    hidden = jax.nn.silu(latent).astype(jnp.bfloat16).reshape(fanout * places, -1)
    message = jnp.dot(hidden, edge_output, preferred_element_type=jnp.float32)
    new_edges = (flat_edges.astype(jnp.float32) + normalize(message, edge_gain, edge_shift)).astype(
        jnp.bfloat16
    )
    new_edges = new_edges.reshape(fanout, places, feature)
    summed = jnp.sum(new_edges.astype(jnp.float32), axis=0).astype(jnp.bfloat16)
    node_hidden = jnp.dot(flat_nodes, node_self, preferred_element_type=jnp.float32)
    node_hidden = (
        node_hidden + jnp.dot(summed, node_summed, preferred_element_type=jnp.float32) + node_bias
    )
    node_hidden = jax.nn.silu(node_hidden).astype(jnp.bfloat16)
    node_message = jnp.dot(node_hidden, node_output, preferred_element_type=jnp.float32)
    new_nodes = (
        flat_nodes.astype(jnp.float32) + normalize(node_message, node_gain, node_shift)
    ).astype(jnp.bfloat16)
    return (
        new_nodes.reshape(height, breadth, feature),
        new_edges.reshape(fanout, height, breadth, feature),
    )


def offset_index(link_codes, reach_cells, padded_breadth):
    window_span = 2 * reach_cells + 1
    row_place = lax.broadcasted_iota(jnp.int32, link_codes.shape, 1)
    col_place = lax.broadcasted_iota(jnp.int32, link_codes.shape, 2)
    return (
        (row_place + link_codes // window_span) * padded_breadth
        + col_place
        + link_codes % window_span
    )


def widen(parent_values, height, breadth):
    parent_rows, parent_cols, feature = parent_values.shape
    spread_out = jnp.broadcast_to(
        parent_values[:, None, :, None, :], (parent_rows, 4, parent_cols, 4, feature)
    )
    return spread_out.reshape(height, breadth, feature)


def assemble_nodes(pieces, across, along):
    total, block_rows, block_cols, feature = pieces.shape
    arranged = pieces.reshape(across, along, block_rows, block_cols, feature).transpose(
        0, 2, 1, 3, 4
    )
    return arranged.reshape(across * block_rows, along * block_cols, feature)


def per_device(
    fine_nodes,
    fine_edges,
    fine_links,
    mid_nodes,
    mid_edges,
    mid_links,
    coarse_nodes,
    coarse_edges,
    coarse_links,
    edge_self,
    edge_sender,
    edge_receiver,
    edge_bias,
    edge_output,
    edge_gain,
    edge_shift,
    node_self,
    node_summed,
    node_bias,
    node_output,
    node_gain,
    node_shift,
    prolongation,
    pooling,
):
    tile_rows, tile_cols, feature = fine_nodes.shape
    mid_rows, mid_cols = (tile_rows // 4, tile_cols // 4)
    block_rows, block_cols = (tile_rows // 16, tile_cols // 16)
    coarse_rows, coarse_cols = (coarse_nodes.shape[0], coarse_nodes.shape[1])
    across = lax.axis_size(DX)
    along = lax.axis_size(DY)
    first_index = lax.axis_index(DX)
    second_index = lax.axis_index(DY)
    row_offset = first_index * block_rows
    col_offset = second_index * block_cols
    zero_offset = jnp.zeros((), jnp.int32)
    weights = tuple(
        (
            stacked[0]
            for stacked in (
                edge_self,
                edge_receiver,
                edge_bias,
                edge_output,
                edge_gain,
                edge_shift,
                node_self,
                node_summed,
                node_bias,
                node_output,
                node_gain,
                node_shift,
            )
        )
    )
    sender_matrix = edge_sender[0]
    fine_rim = with_halo(fine_nodes, ((DX, 0), (DY, 1)), FINE_REACH)
    fine_terms = jnp.dot(
        fine_rim.reshape(-1, feature), sender_matrix, preferred_element_type=jnp.float32
    )
    fine_index = offset_index(fine_links, FINE_REACH, tile_cols + 2 * FINE_REACH)
    fine_new, fine_edges = level_update(fine_nodes, fine_edges, fine_terms, fine_index, weights)
    pooled = (
        mid_nodes.astype(jnp.float32)
        .reshape(block_rows, 4, block_cols, 4, feature)
        .mean(axis=(1, 3))
        .astype(jnp.bfloat16)
    )
    raised = jnp.dot(pooled.reshape(-1, feature), pooling[0], preferred_element_type=jnp.float32)
    own_coarse = lax.dynamic_slice(
        coarse_nodes, (row_offset, col_offset, zero_offset), (block_rows, block_cols, feature)
    )
    own_coarse = (
        own_coarse.astype(jnp.float32) + raised.reshape(block_rows, block_cols, feature)
    ).astype(jnp.bfloat16)
    gathered = gather_axes(own_coarse[None], (("dx_0", "dx_1", "dy_0", "dy_1"), "dy_2"), (0, 1), 0)
    coarse_nodes = assemble_nodes(gathered, across, along)
    coarse_terms = jnp.dot(
        coarse_nodes.reshape(-1, feature), sender_matrix, preferred_element_type=jnp.float32
    )
    coarse_nodes, coarse_edges = level_update(
        coarse_nodes, coarse_edges, coarse_terms, coarse_links, weights
    )
    lifted = jnp.dot(
        coarse_nodes.reshape(-1, feature), prolongation[0], preferred_element_type=jnp.float32
    )
    lifted = lifted.reshape(coarse_rows, coarse_cols, feature)
    mid_source = mid_nodes
    mid_rim = with_halo(mid_source, ((DX, 0), (DY, 1)), MID_REACH)
    row_places = (
        first_index * mid_rows - MID_REACH + jnp.arange(mid_rows + 2 * MID_REACH, dtype=jnp.int32)
    )
    col_places = (
        second_index * mid_cols - MID_REACH + jnp.arange(mid_cols + 2 * MID_REACH, dtype=jnp.int32)
    )
    row_parent = row_places % (coarse_rows * 4) // 4
    col_parent = col_places % (coarse_cols * 4) // 4
    rim_lift = jnp.take(jnp.take(lifted, row_parent, axis=0), col_parent, axis=1)
    mid_rim = (mid_rim.astype(jnp.float32) + rim_lift).astype(jnp.bfloat16)
    mid_nodes = mid_rim[MID_REACH : MID_REACH + mid_rows, MID_REACH : MID_REACH + mid_cols]
    mid_terms = jnp.dot(
        mid_rim.reshape(-1, feature), sender_matrix, preferred_element_type=jnp.float32
    )
    mid_index = offset_index(mid_links, MID_REACH, mid_cols + 2 * MID_REACH)
    mid_nodes, mid_edges = level_update(mid_nodes, mid_edges, mid_terms, mid_index, weights)
    lifted_mid = jnp.dot(
        mid_nodes.reshape(-1, feature), prolongation[0], preferred_element_type=jnp.float32
    )
    lifted_mid = lifted_mid.reshape(mid_rows, mid_cols, feature)
    fine_nodes = (fine_new.astype(jnp.float32) + widen(lifted_mid, tile_rows, tile_cols)).astype(
        jnp.bfloat16
    )
    return (fine_nodes, fine_edges, mid_nodes, mid_edges, coarse_nodes, coarse_edges)


def solution(mesh):
    torus = Mesh(mesh.devices.reshape(2, 4, 2, 4, 2), ("dx_0", "dx_1", "dy_0", "dy_1", "dy_2"))
    in_specs = (
        P(DX, DY, None),
        P(None, DX, DY, None),
        P(None, DX, DY),
        P(DX, DY, None),
        P(None, DX, DY, None),
        P(None, DX, DY),
        P(),
        P(),
        P(),
        P(),
        P(),
        P(),
        P(),
        P(),
        P(),
        P(),
        P(),
        P(),
        P(),
        P(),
        P(),
        P(),
        P(),
        P(),
    )
    out_specs = (
        P(DX, DY, None),
        P(None, DX, DY, None),
        P(DX, DY, None),
        P(None, DX, DY, None),
        P(),
        P(),
    )
    return jax.shard_map(
        per_device, mesh=torus, in_specs=in_specs, out_specs=out_specs, check_vma=False
    )
```

profile of v0, /device:TPU:0, one launch (start us, length us, event | category | flops | bytes accessed | tf_op | source)
XLA Modules:
  0.0 355.0 jit_solution(18027557386560085851)
XLA Ops:
  3.8 2.5 collective-permute-start.1
  7.8 4.1 %collective-permute-start.5 = (bf16[1,4,512]{2,0,1:T(2,128)(2,1)}, bf16[1,4,512]{2,0,1:T(2,128)(2,1)}, u32[]{:S(2)}, u32[]{:S(2)}) collective-permute-start(bf16[1,4,512]{2,0,1:T(2,128)(2,1)} %get-tuple-element.13), channel_id=1, source_target_pairs={{16,0},{32,16},{48,32},{64,48},{80,64},{96,80},{112,96},{0,112},{1... | collective-permute-start | bytes 12296 | tf_op jit(solution)/shard_map/ppermute | solution.py:22
  20.0 176.0 %all-gather = bf16[128,1,512]{2,1,0:T(2,128)(2,1)S(1)} all-gather(bf16[2,1,512]{2,1,0:T(2,128)(2,1)S(1)} %copy.119), channel_id=2, replica_groups=mesh['dx_0'=2,'dx_1'=4,'dy_0'=2,'dy_1'=4,'dy_2'=2] {'dx_0','dx_1','dy_0'..., dimensions={0}, use_global_device_ids=true | all-gather | bytes 133120 | tf_op jit(solution)/shard_map/all_gather | solution.py:36
  196.9 2.2 all_gather.7
  199.5 3.9 %fusion.37 = f32[512,1536]{1,0:T(8,128)} fusion(bf16[512,512]{1,0:T(8,128)(2,1)} %bitcast.175, bf16[1,512,1536]{2,1,0:T(8,128)(2,1)S(1)} %copy-done.1), kind=kOutput, calls=%fused_computation.56 | convolution fusion | flops 805306368 | bytes 5242880 | tf_op jit(solution)/shard_map/dot_general | solution.py:87
  203.4 2.6 convolution_add_fusion.1
  213.2 6.7 %gather_fusion.1 = f32[1536,1536]{1,0:T(8,128)} fusion(f32[256,1536]{1,0:T(8,128)S(1)} %fusion.26, s32[2048]{0:T(1024)S(1)} %pad_clamp_fusion), kind=kCustom, calls=%fused_computation.1 | custom fusion | bytes 18880512 | tf_op jit(solution)/shard_map/jit(_take)/gather | solution.py:78
  219.9 7.3 %multiply_convert_fusion.1 = bf16[6,256,1536]{2,1,0:T(8,128)(2,1)S(1)} fusion(f32[6,256,1536]{2,1,0:T(8,128)} %bitcast.169, bf16[6,256,512]{2,1,0:T(8,128)(2,1)} %bitcast.180, f32[256,1536]{1,0:T(8,128)} %convolution_add_fusion.3, pred[6,256]{1,0:T(8,128)(4,1)S(1)} %compare_and_fusion.1, bf16[1,512,1536]{2,1,0:T(8,128)(2,1)S(1)} %copy-done), kind=kOutput, calls=%fused_computation.6 | convolution fusion | flops 2434793472 | bytes 18875904 | tf_op jit(solution)/shard_map/dot_general | solution.py:74
  227.2 2.7 fusion.86
  233.6 4.4 %fusion.87 = (f32[256]{0:T(256)S(1)}, f32[256,512]{1,0:T(8,128)}) fusion(bf16[1,1536,512]{2,1,0:T(8,128)(2,1)} %param.43, f32[256,1536]{1,0:T(8,128)} %fusion.35, bf16[256,512]{1,0:T(8,128)(2,1)} %reduce_sum.170, bf16[1,512,1536]{2,1,0:T(8,128)(2,1)} %param.41, f32[1536]{0:T(1024)S(1)} %reduce.7), kind=kOutput, calls=%fused_computation.187 | convolution fusion | flops 808189696 | bytes 5512192 | tf_op jit(solution)/shard_map/dot_general | solution.py:92
  244.8 5.2 %collective-permute-start.7 = (bf16[10,1,512]{2,0,1:T(8,128)(2,1)}, bf16[10,1,512]{2,0,1:T(8,128)(2,1)}, u32[]{:S(2)}, u32[]{:S(2)}) collective-permute-start(bf16[10,1,512]{2,0,1:T(8,128)(2,1)} %get-tuple-element.11), channel_id=1, source_target_pairs={{1,0},{2,1},{3,2},{4,3},{5,4},{6,5},{7,6},{8,7},{9,8},{10,9},{11,1... | collective-permute-start | bytes 30728 | tf_op jit(solution)/shard_map/ppermute | solution.py:22
  252.4 2.5 gather_fusion.3
  258.7 2.5 convolution_add_fusion.6
  268.9 2.7 fusion.91
  275.3 5.4 %collective-permute-start.3 = (bf16[38,3,512]{2,1,0:T(4,128)(2,1)}, bf16[38,3,512]{2,1,0:T(4,128)(2,1)S(1)}, u32[]{:S(2)}, u32[]{:S(2)}) collective-permute-start(bf16[38,3,512]{2,1,0:T(4,128)(2,1)} %get-tuple-element.7), channel_id=1, source_target_pairs={{1,0},{2,1},{3,2},{4,3},{5,4},{6,5},{7,6},{8,7},{9,8},{10,9},{11,1... | collective-permute-start | bytes 350216 | tf_op jit(solution)/shard_map/ppermute | solution.py:22
  283.8 2.6 pad_maximum_fusion
  286.3 2.1 reshape.524
  288.5 5.0 %fusion.28 = f32[836,1536]{1,0:T(8,128)} fusion(bf16[836,512]{1,0:T(8,128)(2,1)} %reshape.524, bf16[1,512,1536]{2,1,0:T(8,128)(2,1)S(1)} %copy-done.4), kind=kOutput, calls=%fused_computation.47 | convolution fusion | flops 1314914304 | bytes 7565312 | tf_op jit(solution)/shard_map/dot_general | solution.py:187
  293.5 23.1 %gather_fusion = f32[3072,1536]{1,0:T(8,128)} fusion(f32[836,1536]{1,0:T(8,128)} %fusion.28, s32[3072]{0:T(1024)S(1)} %copy-done.26), kind=kCustom, calls=%fused_computation | custom fusion | bytes 37761024 | tf_op jit(solution)/shard_map/jit(_take)/gather | solution.py:78
  316.6 14.7 %multiply_convert_fusion = bf16[6,512,1536]{2,1,0:T(8,128)(2,1)} fusion(f32[6,512,1536]{2,1,0:T(8,128)} %bitcast.166, f32[512,1536]{1,0:T(8,128)} %convolution_add_fusion.1, pred[6,512]{1,0:T(8,128)(4,1)S(1)} %copy-done.43, bf16[6,512,512]{2,1,0:T(8,128)(2,1)} %bitcast.177, bf16[1,512,1536]{2,1,0:T(8,128)(2,1)S(1)} %copy-done), kind=kOutput, calls=%fused_computation.5 | convolution fusion | flops 4869586944 | bytes 36178944 | tf_op jit(solution)/shard_map/dot_general | solution.py:74
  331.3 7.9 %fusion.94 = (f32[3072]{0:T(1024)S(1)}, f32[3072,512]{1,0:T(8,128)S(1)}) fusion(bf16[3072,1536]{1,0:T(8,128)(2,1)} %bitcast.200, bf16[1,1536,512]{2,1,0:T(8,128)(2,1)S(1)} %copy-done.15), kind=kOutput, calls=%fused_computation.190 | convolution fusion | flops 4833408000 | bytes 17313792 | tf_op jit(solution)/shard_map/dot_general | solution.py:81
  341.4 3.0 fusion
  344.4 3.3 reduce_sum.162
  347.7 5.1 %fusion.95 = (f32[512]{0:T(512)S(1)}, f32[512,512]{1,0:T(8,128)S(1)}) fusion(bf16[1,1536,512]{2,1,0:T(8,128)(2,1)} %param.43, f32[512,1536]{1,0:T(8,128)} %fusion.37, bf16[512,512]{1,0:T(8,128)(2,1)} %reduce_sum.162, bf16[1,512,1536]{2,1,0:T(8,128)(2,1)} %param.41, f32[1536]{0:T(1024)S(1)} %reduce.7), kind=kOutput, calls=%fused_computation.191 | convolution fusion | flops 1616379392 | bytes 7872512 | tf_op jit(solution)/shard_map/dot_general | solution.py:92
  (201 shorter events, 56.1 us)
Async XLA Ops:
  0.6 219.2 %copy-start = (bf16[1,512,1536]{2,1,0:T(8,128)(2,1)S(1)}, bf16[1,512,1536]{2,1,0:T(8,128)(2,1)}, u32[]{:S(2)}) copy-start(bf16[1,512,1536]{2,1,0:T(8,128)(2,1)} %param.33) | copy-start | bytes 4718596
  2.2 269.7 %collective-permute-start = (bf16[3,16,512]{2,1,0:T(8,128)(2,1)}, bf16[3,16,512]{2,1,0:T(8,128)(2,1)}, u32[]{:S(2)}, u32[]{:S(2)}) collective-permute-start(bf16[3,16,512]{2,1,0:T(8,128)(2,1)} %get-tuple-element.9), channel_id=1, source_target_pairs={{0,16},{16,32},{32,48},{48,64},{64,80},{80,96},{96,112},{112,0},{1... | collective-permute-start | bytes 147464 | tf_op jit(solution)/shard_map/ppermute | solution.py:21
  3.8 269.0 %collective-permute-start.1 = (bf16[3,16,512]{2,1,0:T(8,128)(2,1)}, bf16[3,16,512]{2,1,0:T(8,128)(2,1)}, u32[]{:S(2)}, u32[]{:S(2)}) collective-permute-start(bf16[3,16,512]{2,1,0:T(8,128)(2,1)} %get-tuple-element.8), channel_id=1, source_target_pairs={{16,0},{32,16},{48,32},{64,48},{80,64},{96,80},{112,96},{0,112},{1... | collective-permute-start | bytes 147464 | tf_op jit(solution)/shard_map/ppermute | solution.py:22
  7.8 235.6 %collective-permute-start.4 = (bf16[1,4,512]{2,0,1:T(2,128)(2,1)}, bf16[1,4,512]{2,0,1:T(2,128)(2,1)}, u32[]{:S(2)}, u32[]{:S(2)}) collective-permute-start(bf16[1,4,512]{2,0,1:T(2,128)(2,1)} %get-tuple-element.12), channel_id=1, source_target_pairs={{0,16},{16,32},{32,48},{48,64},{64,80},{80,96},{96,112},{112,0},{1... | collective-permute-start | bytes 12296 | tf_op jit(solution)/shard_map/ppermute | solution.py:21
  7.8 235.6 %collective-permute-start.5 = (bf16[1,4,512]{2,0,1:T(2,128)(2,1)}, bf16[1,4,512]{2,0,1:T(2,128)(2,1)}, u32[]{:S(2)}, u32[]{:S(2)}) collective-permute-start(bf16[1,4,512]{2,0,1:T(2,128)(2,1)} %get-tuple-element.13), channel_id=1, source_target_pairs={{16,0},{32,16},{48,32},{64,48},{80,64},{96,80},{112,96},{0,112},{1... | collective-permute-start | bytes 12296 | tf_op jit(solution)/shard_map/ppermute | solution.py:22
  20.0 179.4 %copy-start.41 = (f32[1,1536]{1,0:T(1,128)S(1)}, f32[1,1536]{1,0:T(1,128)}, u32[]{:S(2)}) copy-start(f32[1,1536]{1,0:T(1,128)} %param.36) | copy-start | bytes 18436
  20.0 179.4 %copy-start.1 = (bf16[1,512,1536]{2,1,0:T(8,128)(2,1)S(1)}, bf16[1,512,1536]{2,1,0:T(8,128)(2,1)}, u32[]{:S(2)}) copy-start(bf16[1,512,1536]{2,1,0:T(8,128)(2,1)} %param.40) | copy-start | bytes 4718596
  219.9 7.3 %copy-start.13 = (bf16[1,1536,512]{2,1,0:T(8,128)(2,1)S(1)}, bf16[1,1536,512]{2,1,0:T(8,128)(2,1)}, u32[]{:S(2)}) copy-start(bf16[1,1536,512]{2,1,0:T(8,128)(2,1)} %param.37) | copy-start | bytes 4718596
  232.3 5.6 %copy-start.5 = (bf16[1536,512]{1,0:T(8,128)(2,1)}, bf16[1536,512]{1,0:T(8,128)(2,1)S(1)}, u32[]{:S(2)}) copy-start(bf16[1536,512]{1,0:T(8,128)(2,1)S(1)} %fusion.2) | copy-start | bytes 4718596
  233.5 6.3 %copy-start.35 = (f32[1,512]{1,0:T(1,128)S(1)}, f32[1,512]{1,0:T(1,128)}, u32[]{:S(2)}) copy-start(f32[1,512]{1,0:T(1,128)} %param.45) | copy-start | bytes 6148
  233.5 6.3 %copy-start.37 = (f32[1,512]{1,0:T(1,128)S(1)}, f32[1,512]{1,0:T(1,128)}, u32[]{:S(2)}) copy-start(f32[1,512]{1,0:T(1,128)} %param.44) | copy-start | bytes 6148
  241.1 9.5 %copy-start.20 = (bf16[6,8,4,512]{3,2,1,0:T(4,128)(2,1)S(1)}, bf16[6,8,4,512]{3,2,1,0:T(4,128)(2,1)}, u32[]{:S(2)}) copy-start(bf16[6,8,4,512]{3,2,1,0:T(4,128)(2,1)} %param.28) | copy-start | bytes 589828
  244.7 10.2 %collective-permute-start.6 = (bf16[10,1,512]{2,0,1:T(8,128)(2,1)}, bf16[10,1,512]{2,0,1:T(8,128)(2,1)}, u32[]{:S(2)}, u32[]{:S(2)}) collective-permute-start(bf16[10,1,512]{2,0,1:T(8,128)(2,1)} %get-tuple-element.10), channel_id=1, source_target_pairs={{0,1},{1,2},{2,3},{3,4},{4,5},{5,6},{6,7},{7,8},{8,9},{9,10},{10,1... | collective-permute-start | bytes 30728 | tf_op jit(solution)/shard_map/ppermute | solution.py:21
  244.8 10.1 %collective-permute-start.7 = (bf16[10,1,512]{2,0,1:T(8,128)(2,1)}, bf16[10,1,512]{2,0,1:T(8,128)(2,1)}, u32[]{:S(2)}, u32[]{:S(2)}) collective-permute-start(bf16[10,1,512]{2,0,1:T(8,128)(2,1)} %get-tuple-element.11), channel_id=1, source_target_pairs={{1,0},{2,1},{3,2},{4,3},{5,4},{6,5},{7,6},{8,7},{9,8},{10,9},{11,1... | collective-permute-start | bytes 30728 | tf_op jit(solution)/shard_map/ppermute | solution.py:22
  252.4 8.7 %copy-start.2 = (bf16[1,512,1536]{2,1,0:T(8,128)(2,1)S(1)}, bf16[1,512,1536]{2,1,0:T(8,128)(2,1)}, u32[]{:S(2)}) copy-start(bf16[1,512,1536]{2,1,0:T(8,128)(2,1)} %param.40) | copy-start | bytes 4718596
  271.6 9.1 %copy-start.12 = (bf16[1,512,512]{2,1,0:T(8,128)(2,1)S(1)}, bf16[1,512,512]{2,1,0:T(8,128)(2,1)}, u32[]{:S(2)}) copy-start(bf16[1,512,512]{2,1,0:T(8,128)(2,1)} %param.46) | copy-start | bytes 1572868
  271.9 9.9 %copy-start.25 = (bf16[8,4,512]{2,1,0:T(4,128)(2,1)}, bf16[8,4,512]{2,1,0:T(4,128)(2,1)S(1)}, u32[]{:S(2)}) copy-start(bf16[8,4,512]{2,1,0:T(4,128)(2,1)S(1)} %reshape.539) | copy-start | bytes 98308
  275.3 8.5 %collective-permute-start.2 = (bf16[38,3,512]{2,1,0:T(4,128)(2,1)}, bf16[38,3,512]{2,1,0:T(4,128)(2,1)S(1)}, u32[]{:S(2)}, u32[]{:S(2)}) collective-permute-start(bf16[38,3,512]{2,1,0:T(4,128)(2,1)} %get-tuple-element.6), channel_id=1, source_target_pairs={{0,1},{1,2},{2,3},{3,4},{4,5},{5,6},{6,7},{7,8},{8,9},{9,10},{10,1... | collective-permute-start | bytes 350216 | tf_op jit(solution)/shard_map/ppermute | solution.py:21
  275.3 8.5 %collective-permute-start.3 = (bf16[38,3,512]{2,1,0:T(4,128)(2,1)}, bf16[38,3,512]{2,1,0:T(4,128)(2,1)S(1)}, u32[]{:S(2)}, u32[]{:S(2)}) collective-permute-start(bf16[38,3,512]{2,1,0:T(4,128)(2,1)} %get-tuple-element.7), channel_id=1, source_target_pairs={{1,0},{2,1},{3,2},{4,3},{5,4},{6,5},{7,6},{8,7},{9,8},{10,9},{11,1... | collective-permute-start | bytes 350216 | tf_op jit(solution)/shard_map/ppermute | solution.py:22
  283.2 5.3 %copy-start.4 = (bf16[1,512,1536]{2,1,0:T(8,128)(2,1)S(1)}, bf16[1,512,1536]{2,1,0:T(8,128)(2,1)}, u32[]{:S(2)}) copy-start(bf16[1,512,1536]{2,1,0:T(8,128)(2,1)} %param.34) | copy-start | bytes 4718596
  288.5 5.0 %copy-start.26 = (s32[3072]{0:T(1024)S(1)}, s32[3072]{0:T(1024)}, u32[]{:S(2)}) copy-start(s32[3072]{0:T(1024)} %broadcast_clamp_fusion) | copy-start | bytes 36868
  293.5 23.1 %copy-start.43 = (pred[6,512]{1,0:T(8,128)(4,1)S(1)}, pred[6,512]{1,0:T(8,128)(4,1)}, u32[]{:S(2)}) copy-start(pred[6,512]{1,0:T(8,128)(4,1)} %compare_and_fusion) | copy-start | bytes 9220
  316.6 14.7 %copy-start.15 = (bf16[1,1536,512]{2,1,0:T(8,128)(2,1)S(1)}, bf16[1,1536,512]{2,1,0:T(8,128)(2,1)}, u32[]{:S(2)}) copy-start(bf16[1,1536,512]{2,1,0:T(8,128)(2,1)} %param.37) | copy-start | bytes 4718596
  347.7 5.4 %copy-start.8 = (bf16[32,16,512]{2,1,0:T(8,128)(2,1)S(1)}, bf16[32,16,512]{2,1,0:T(8,128)(2,1)}, u32[]{:S(2)}) copy-start(bf16[32,16,512]{2,1,0:T(8,128)(2,1)} %param.24) | copy-start | bytes 1572868
  (29 other events, 66.2 us)
where the time goes:
time: 356 us; the launch traced here: 355 us
  blocking collectives  178 us (50%)
  matrix products  71 us (20%)
  local copies, waits for them, and re-layouts  57.6 us (16%)
  other arithmetic  27.2 us (8%)
  starting transfers between devices  19 us (5%)
    all_gather x2, blocking collectives, all_blocks(): blocks = lax.all_gather(blocks, axes[k], axis=0, tiled=True)  178 us
    gather x3, local copies, waits for them, and re-layouts, level_update(): jnp.take(sender_terms, senders.reshape(fanout, places), axis=0)  30.9 us
    dot_general x3, matrix products, level_update(): jnp.dot(flat_edges, self_matrix, preferred_element_type=jnp.float32)  23.7 us
    ppermute x4, starting transfers between devices, with_halo(): after = lax.ppermute(leading, axis, down)  17.2 us
    dot_general x3, matrix products, level_update(): jnp.dot(node_hidden, node_output, preferred_element_type=jnp.float32)  12.2 us
    dot_general x3, matrix products, level_update(): message = jnp.dot(hidden, edge_output, preferred_element_type=jnp.float32)  11.1 us
  transfers between devices with their start and end apart: 8, of which 1 were waited for; matrix products, arithmetic and copies ran while one was open for 22% of the time, Pallas kernels for 0%

commit v1 on v0

--- a/solution.py
+++ b/solution.py
@@ -33,7 +33,10 @@
 def all_blocks(value, axes, turns):
     blocks = value[None]
     for k in turns:
-        blocks = lax.all_gather(blocks, axes[k], axis=0, tiled=True)
+        arr_in = axes[k]
+        blocks = jnp.concatenate(
+            lax.all_to_all(jnp.stack([blocks] * lax.axis_size(arr_in), axis=0), arr_in, 0, 0), 0
+        )
     block = [lax.axis_size(axes[k]) for k in reversed(turns)]
     blocks = blocks.reshape(*block, *value.shape)
     turned = sorted(range(len(turns)), key=lambda place: turns[len(turns) - 1 - place])

time: 356 us -> 187 us (0.53)
  blocking collectives: 178 us -> 4.08 us
  starting transfers between devices: 19 us -> 28.4 us
  local copies, waits for them, and re-layouts: 57.6 us -> 52.8 us
    all_gather x2 -> x0, blocking collectives: 178 us -> none  [all_blocks(): blocks = lax.all_gather(blocks, axes[k], axis=0, tiled=True)]
    all_to_all x0 -> x1, starting transfers between devices: none -> 9.42 us  [all_blocks(): lax.all_to_all(jnp.stack([blocks] * lax.axis_size(arr_in), axis=0), arr_i...]
    all_to_all x0 -> x1, blocking collectives: none -> 4.08 us  [all_blocks(): lax.all_to_all(jnp.stack([blocks] * lax.axis_size(arr_in), axis=0), arr_i...]
    reshape x6, local copies, waits for them, and re-layouts: 4.53 us -> 0.53 us  [level_update(): senders.reshape(fanout, places)]
  transfers between devices with their start and end apart: 8 -> 9, of which waited for: 1 -> 0; matrix products, arithmetic and copies ran while one was open for 22% -> 41% of each run, Pallas kernels for 0% -> 0%
where the time goes in v1:
time: 187 us; the launch traced here: 185 us
  matrix products  69.2 us (37%)
  local copies, waits for them, and re-layouts  52.8 us (28%)
  other arithmetic  29 us (16%)
  starting transfers between devices  28.4 us (15%)
  blocking collectives  4.08 us (2%)
    gather x3, local copies, waits for them, and re-layouts, level_update(): jnp.take(sender_terms, senders.reshape(fanout, places), axis=0)  31 us
    dot_general x3, matrix products, level_update(): jnp.dot(flat_edges, self_matrix, preferred_element_type=jnp.float32)  23.7 us
    ppermute x4, starting transfers between devices, with_halo(): after = lax.ppermute(leading, axis, down)  15.8 us
    dot_general x3, matrix products, level_update(): jnp.dot(node_hidden, node_output, preferred_element_type=jnp.float32)  12.2 us
    dot_general x3, matrix products, level_update(): message = jnp.dot(hidden, edge_output, preferred_element_type=jnp.float32)  11.4 us
    all_to_all x1, starting transfers between devices, all_blocks(): lax.all_to_all(jnp.stack([blocks] * lax.axis_size(arr_in), axis=0), arr_i...  9.42 us
    dot_general x3, matrix products, level_update(): jnp.dot(flat_nodes, receiver_matrix, preferred_element_type=jnp.float32)  6.83 us
    dot_general x3, matrix products, level_update(): jnp.dot(flat_nodes, node_self, preferred_element_type=jnp.float32)  6.03 us
  transfers between devices with their start and end apart: 9, of which 0 were waited for; matrix products, arithmetic and copies ran while one was open for 41% of the time, Pallas kernels for 0%

profile of v1, /device:TPU:0, one launch (start us, length us, event | category | flops | bytes accessed | tf_op | source)
XLA Modules:
  0.0 184.8 jit_solution(5254437568697045630)
XLA Ops:
  3.9 2.5 %collective-permute-start.1 = (bf16[3,16,512]{2,1,0:T(8,128)(2,1)}, bf16[3,16,512]{2,1,0:T(8,128)(2,1)}, u32[]{:S(2)}, u32[]{:S(2)}) collective-permute-start(bf16[3,16,512]{2,1,0:T(8,128)(2,1)} %get-tuple-element.8), channel_id=1, source_target_pairs={{16,0},{32,16},{48,32},{64,48},{80,64},{96,80},{112,96},{0,112},{1... | collective-permute-start | bytes 147464 | tf_op jit(solution)/shard_map/ppermute | solution.py:22
  10.0 9.4 %all-to-all-start = ((bf16[64,1,1,2,1,512]{5,3,4,2,1,0:T(2,128)(2,1)}), bf16[64,1,1,2,1,512]{5,3,4,2,1,0:T(2,128)(2,1)S(1)}, u32[]{:S(2)}, u32[]{:S(2)}) async-start(bf16[64,1,1,2,1,512]{5,3,4,2,1,0:T(2,128)(2,1)} %stack.6), calls=%async_computation | async-start | bytes 262144 | tf_op jit(solution)/shard_map/all_to_all | solution.py:38
  22.3 2.6 %collective-permute-start.5 = (bf16[1,4,512]{2,0,1:T(2,128)(2,1)}, bf16[1,4,512]{2,0,1:T(2,128)(2,1)}, u32[]{:S(2)}, u32[]{:S(2)}) collective-permute-start(bf16[1,4,512]{2,0,1:T(2,128)(2,1)} %get-tuple-element.13), channel_id=1, source_target_pairs={{16,0},{32,16},{48,32},{64,48},{80,64},{96,80},{112,96},{0,112},{1... | collective-permute-start | bytes 12296 | tf_op jit(solution)/shard_map/ppermute | solution.py:22
  30.9 3.9 %fusion.37 = f32[512,1536]{1,0:T(8,128)} fusion(bf16[512,512]{1,0:T(8,128)(2,1)} %bitcast.179, bf16[1,512,1536]{2,1,0:T(8,128)(2,1)S(1)} %copy-done.1), kind=kOutput, calls=%fused_computation.56 | convolution fusion | flops 805306368 | bytes 5242880 | tf_op jit(solution)/shard_map/dot_general | solution.py:90
  34.9 2.6 %convolution_add_fusion.1 = f32[512,1536]{1,0:T(8,128)} fusion(bf16[512,512]{1,0:T(8,128)(2,1)S(1)} %bitcast.180, bf16[1,512,1536]{2,1,0:T(8,128)(2,1)S(1)} %copy-done.3, f32[1536]{0:T(1024)S(1)} %reduce.6), kind=kOutput, calls=%fused_computation.12 | convolution fusion | flops 806092800 | bytes 5249024 | tf_op jit(solution)/shard_map/dot_general | solution.py:76
  42.2 5.4 %collective-permute-start.7 = (bf16[10,1,512]{2,0,1:T(8,128)(2,1)}, bf16[10,1,512]{2,0,1:T(8,128)(2,1)}, u32[]{:S(2)}, u32[]{:S(2)}) collective-permute-start(bf16[10,1,512]{2,0,1:T(8,128)(2,1)} %get-tuple-element.11), channel_id=1, source_target_pairs={{1,0},{2,1},{3,2},{4,3},{5,4},{6,5},{7,6},{8,7},{9,8},{10,9},{11,1... | collective-permute-start | bytes 30728 | tf_op jit(solution)/shard_map/ppermute | solution.py:22
  51.9 5.4 %collective-permute-start.3 = (bf16[38,3,512]{2,1,0:T(4,128)(2,1)}, bf16[38,3,512]{2,1,0:T(4,128)(2,1)}, u32[]{:S(2)}, u32[]{:S(2)}) collective-permute-start(bf16[38,3,512]{2,1,0:T(4,128)(2,1)} %get-tuple-element.7), channel_id=1, source_target_pairs={{1,0},{2,1},{3,2},{4,3},{5,4},{6,5},{7,6},{8,7},{9,8},{10,9},{11,1... | collective-permute-start | bytes 350216 | tf_op jit(solution)/shard_map/ppermute | solution.py:22
  57.3 4.1 %all_to_all.10 = bf16[2,64,1,2,1,512]{5,1,4,3,2,0:T(8,128)(2,1)S(1)} all-to-all(bf16[2,64,1,2,1,512]{5,1,4,3,2,0:T(8,128)(2,1)S(1)} %pad_maximum_fusion.1), channel_id=1, replica_groups=mesh['dx_0'=2,'dx_1'=4,'dy_0'=2,'dy_1'=4,'dy_2'=2] {'dy_2'}, dimensions={0} | all-to-all | bytes 524288 | tf_op jit(solution)/shard_map/all_to_all | solution.py:38
  65.7 6.7 %gather_fusion.1 = f32[1536,1536]{1,0:T(8,128)} fusion(f32[256,1536]{1,0:T(8,128)S(1)} %fusion.26, s32[2048]{0:T(1024)S(1)} %pad_clamp_fusion), kind=kCustom, calls=%fused_computation.1 | custom fusion | bytes 18880512 | tf_op jit(solution)/shard_map/jit(_take)/gather | solution.py:81
  72.4 7.3 %multiply_convert_fusion.1 = bf16[6,256,1536]{2,1,0:T(8,128)(2,1)S(1)} fusion(f32[6,256,1536]{2,1,0:T(8,128)} %bitcast.173, bf16[6,256,512]{2,1,0:T(8,128)(2,1)} %bitcast.184, f32[256,1536]{1,0:T(8,128)} %convolution_add_fusion.3, pred[6,256]{1,0:T(8,128)(4,1)S(1)} %copy-done.30, bf16[1,512,1536]{2,1,0:T(8,128)(2,1)S(1)} %copy-done), kind=kOutput, calls=%fused_computation.6 | convolution fusion | flops 2434793472 | bytes 18875904 | tf_op jit(solution)/shard_map/dot_general | solution.py:77
  79.7 2.7 %fusion.87 = (f32[1536]{0:T(1024)S(1)}, f32[1536,512]{1,0:T(8,128)S(1)}) fusion(bf16[1536,1536]{1,0:T(8,128)(2,1)S(1)} %bitcast.205, bf16[1,1536,512]{2,1,0:T(8,128)(2,1)S(1)} %copy-done.14), kind=kOutput, calls=%fused_computation.189 | convolution fusion | flops 2416704000 | bytes 9443328 | tf_op jit(solution)/shard_map/dot_general | solution.py:84
  86.3 4.4 %fusion.88 = (f32[256]{0:T(256)S(1)}, f32[256,512]{1,0:T(8,128)}) fusion(bf16[1,1536,512]{2,1,0:T(8,128)(2,1)} %param.43, f32[256,1536]{1,0:T(8,128)} %fusion.35, bf16[256,512]{1,0:T(8,128)(2,1)} %reduce_sum.170, bf16[1,512,1536]{2,1,0:T(8,128)(2,1)} %param.41, f32[1536]{0:T(1024)S(1)} %reduce.7), kind=kOutput, calls=%fused_computation.190 | convolution fusion | flops 808189696 | bytes 5512192 | tf_op jit(solution)/shard_map/dot_general | solution.py:95
  98.8 2.5 %convolution_add_fusion.6 = f32[32,1536]{1,0:T(8,128)} fusion(bf16[32,512]{1,0:T(8,128)(2,1)S(1)} %reshape.533, bf16[1,512,1536]{2,1,0:T(8,128)(2,1)} %param.35, f32[1536]{0:T(1024)S(1)} %reduce.6), kind=kOutput, calls=%fused_computation.24 | convolution fusion | flops 50380800 | bytes 1808384 | tf_op jit(solution)/shard_map/dot_general | solution.py:76
  107.4 2.7 %fusion.92 = (f32[32]{0:T(128)S(1)}, f32[32,512]{1,0:T(8,128)S(1)}) fusion(bf16[1,1536,512]{2,1,0:T(8,128)(2,1)} %param.43, f32[32,1536]{1,0:T(8,128)S(1)} %fusion.33, bf16[32,512]{1,0:T(8,128)(2,1)S(1)} %reduce_sum.175, bf16[1,512,1536]{2,1,0:T(8,128)(2,1)} %param.41, f32[1536]{0:T(1024)S(1)} %reduce.7), kind=kOutput, calls=%fused_computation.192 | convolution fusion | flops 101023712 | bytes 3446912 | tf_op jit(solution)/shard_map/dot_general | solution.py:95
  113.0 2.7 %pad_maximum_fusion = bf16[38,22,512]{2,1,0:T(8,128)(2,1)} fusion(bf16[38,3,512]{2,1,0:T(4,128)(2,1)} %collective-permute-done.3, bf16[38,16,512]{2,1,0:T(8,128)(2,1)} %copy-done.19, bf16[38,3,512]{2,1,0:T(4,128)(2,1)} %collective-permute-done.2), kind=kLoop, calls=%fused_computation.68 | loop fusion | flops 2568192 | bytes 1712128 | tf_op jit(solution)/shard_map/concatenate | solution.py:23
  115.8 2.1 %reshape.524 = bf16[836,512]{1,0:T(8,128)(2,1)} reshape(bf16[38,22,512]{2,1,0:T(8,128)(2,1)} %pad_maximum_fusion) | data formatting | bytes 1712128 | tf_op jit(solution)/shard_map/reshape | solution.py:191
  117.9 5.0 %fusion.28 = f32[836,1536]{1,0:T(8,128)} fusion(bf16[836,512]{1,0:T(8,128)(2,1)} %reshape.524, bf16[1,512,1536]{2,1,0:T(8,128)(2,1)S(1)} %copy-done.6), kind=kOutput, calls=%fused_computation.47 | convolution fusion | flops 1314914304 | bytes 7565312 | tf_op jit(solution)/shard_map/dot_general | solution.py:190
  122.9 23.2 %gather_fusion = f32[3072,1536]{1,0:T(8,128)} fusion(f32[836,1536]{1,0:T(8,128)} %fusion.28, s32[3072]{0:T(1024)S(1)} %broadcast_clamp_fusion), kind=kCustom, calls=%fused_computation | custom fusion | bytes 37761024 | tf_op jit(solution)/shard_map/jit(_take)/gather | solution.py:81
  146.1 14.7 %multiply_convert_fusion = bf16[6,512,1536]{2,1,0:T(8,128)(2,1)} fusion(f32[6,512,1536]{2,1,0:T(8,128)} %bitcast.170, f32[512,1536]{1,0:T(8,128)} %convolution_add_fusion.1, pred[6,512]{1,0:T(8,128)(4,1)S(1)} %copy-done.29, bf16[6,512,512]{2,1,0:T(8,128)(2,1)} %bitcast.181, bf16[1,512,1536]{2,1,0:T(8,128)(2,1)S(1)} %copy-done), kind=kOutput, calls=%fused_computation.5 | convolution fusion | flops 4869586944 | bytes 36178944 | tf_op jit(solution)/shard_map/dot_general | solution.py:77
  160.9 8.1 %fusion.95 = (f32[3072]{0:T(1024)S(1)}, f32[3072,512]{1,0:T(8,128)S(1)}) fusion(bf16[3072,1536]{1,0:T(8,128)(2,1)} %bitcast.204, bf16[1,1536,512]{2,1,0:T(8,128)(2,1)S(1)} %copy-done.16), kind=kOutput, calls=%fused_computation.193 | convolution fusion | flops 4833408000 | bytes 17313792 | tf_op jit(solution)/shard_map/dot_general | solution.py:84
  169.0 2.1 %multiply_reduce_fusion = f32[3072]{0:T(1024)S(1)} fusion(f32[3072,512]{1,0:T(8,128)S(1)} %get-tuple-element.23, f32[3072]{0:T(1024)S(1)} %broadcast_multiply_fusion), kind=kLoop, calls=%fused_computation.9 | loop fusion | flops 4715520 | bytes 6316032 | tf_op jit(solution)/shard_map/reduce_sum | solution.py:53
  171.2 3.0 %fusion = bf16[3072,512]{1,0:T(8,128)(2,1)} fusion(f32[3072,512]{1,0:T(8,128)S(1)} %get-tuple-element.23, bf16[6,32,16,512]{3,2,1,0:T(8,128)(2,1)S(1)} %copy-done.11, f32[512]{0:T(512)S(1)} %bitcast.194, f32[512]{0:T(512)S(1)} %bitcast.197, f32[3072]{0:T(1024)S(1)} %add_rsqrt_fusion, f32[3072]{0:T(1024)S(1)} %broadcast_multiply_fusion), kind=kLoop, calls=%fused_computation.8 | loop fusion | flops 11010048 | bytes 12611584 | tf_op jit(solution)/shard_map/convert_element_type | solution.py:85
  174.2 3.3 %reduce_sum.162 = bf16[512,512]{1,0:T(8,128)(2,1)} reduce(bf16[6,512,512]{2,1,0:T(8,128)(2,1)} %bitcast.171, bf16[]{:T(256)} %constant.214.clone.1), dimensions={0}, to_apply=%region_2.3 | reduce | flops 1310720 | bytes 3670018 | tf_op jit(solution)/shard_map/reduce_sum | solution.py:89
  177.5 5.1 %fusion.96 = (f32[512]{0:T(512)S(1)}, f32[512,512]{1,0:T(8,128)S(1)}) fusion(bf16[1,1536,512]{2,1,0:T(8,128)(2,1)} %param.43, f32[512,1536]{1,0:T(8,128)} %fusion.37, bf16[512,512]{1,0:T(8,128)(2,1)} %reduce_sum.162, bf16[1,512,1536]{2,1,0:T(8,128)(2,1)} %param.41, f32[1536]{0:T(1024)S(1)} %reduce.7), kind=kOutput, calls=%fused_computation.194 | convolution fusion | flops 1616379392 | bytes 7872512 | tf_op jit(solution)/shard_map/dot_general | solution.py:95
  (181 shorter events, 51.9 us)
Async XLA Ops:
  0.6 71.8 %copy-start = (bf16[1,512,1536]{2,1,0:T(8,128)(2,1)S(1)}, bf16[1,512,1536]{2,1,0:T(8,128)(2,1)}, u32[]{:S(2)}) copy-start(bf16[1,512,1536]{2,1,0:T(8,128)(2,1)} %param.33) | copy-start | bytes 4718596
  0.6 25.4 %copy-start.22 = (s32[6,16,16]{2,1,0:T(8,128)S(1)}, s32[6,16,16]{2,1,0:T(8,128)}, u32[]{:S(2)}) copy-start(s32[6,16,16]{2,1,0:T(8,128)} %param.32) | copy-start | bytes 18436
  0.7 26.7 %copy-start.28 = (s32[6,8,4]{1,2,0:T(4,128)S(1)}, s32[6,8,4]{1,2,0:T(4,128)}, u32[]{:S(2)}) copy-start(s32[6,8,4]{1,2,0:T(4,128)} %param.29) | copy-start | bytes 2308
  0.7 30.2 %copy-start.1 = (bf16[1,512,1536]{2,1,0:T(8,128)(2,1)S(1)}, bf16[1,512,1536]{2,1,0:T(8,128)(2,1)}, u32[]{:S(2)}) copy-start(bf16[1,512,1536]{2,1,0:T(8,128)(2,1)} %param.40) | copy-start | bytes 4718596
  2.3 45.2 %collective-permute-start = (bf16[3,16,512]{2,1,0:T(8,128)(2,1)}, bf16[3,16,512]{2,1,0:T(8,128)(2,1)}, u32[]{:S(2)}, u32[]{:S(2)}) collective-permute-start(bf16[3,16,512]{2,1,0:T(8,128)(2,1)} %get-tuple-element.9), channel_id=1, source_target_pairs={{0,16},{16,32},{32,48},{48,64},{64,80},{80,96},{96,112},{112,0},{1... | collective-permute-start | bytes 147464 | tf_op jit(solution)/shard_map/ppermute | solution.py:21
  3.9 45.5 %collective-permute-start.1 = (bf16[3,16,512]{2,1,0:T(8,128)(2,1)}, bf16[3,16,512]{2,1,0:T(8,128)(2,1)}, u32[]{:S(2)}, u32[]{:S(2)}) collective-permute-start(bf16[3,16,512]{2,1,0:T(8,128)(2,1)} %get-tuple-element.8), channel_id=1, source_target_pairs={{16,0},{32,16},{48,32},{64,48},{80,64},{96,80},{112,96},{0,112},{1... | collective-permute-start | bytes 147464 | tf_op jit(solution)/shard_map/ppermute | solution.py:22
  10.0 47.3 %all-to-all-start = ((bf16[64,1,1,2,1,512]{5,3,4,2,1,0:T(2,128)(2,1)}), bf16[64,1,1,2,1,512]{5,3,4,2,1,0:T(2,128)(2,1)S(1)}, u32[]{:S(2)}, u32[]{:S(2)}) async-start(bf16[64,1,1,2,1,512]{5,3,4,2,1,0:T(2,128)(2,1)} %stack.6), calls=%async_computation | async-start | bytes 262144 | tf_op jit(solution)/shard_map/all_to_all | solution.py:38
  20.8 20.1 %collective-permute-start.4 = (bf16[1,4,512]{2,0,1:T(2,128)(2,1)}, bf16[1,4,512]{2,0,1:T(2,128)(2,1)S(1)}, u32[]{:S(2)}, u32[]{:S(2)}) collective-permute-start(bf16[1,4,512]{2,0,1:T(2,128)(2,1)} %get-tuple-element.12), channel_id=1, source_target_pairs={{0,16},{16,32},{32,48},{48,64},{64,80},{80,96},{96,112},{112,0},{1... | collective-permute-start | bytes 12296 | tf_op jit(solution)/shard_map/ppermute | solution.py:21
  22.3 18.5 %collective-permute-start.5 = (bf16[1,4,512]{2,0,1:T(2,128)(2,1)}, bf16[1,4,512]{2,0,1:T(2,128)(2,1)}, u32[]{:S(2)}, u32[]{:S(2)}) collective-permute-start(bf16[1,4,512]{2,0,1:T(2,128)(2,1)} %get-tuple-element.13), channel_id=1, source_target_pairs={{16,0},{32,16},{48,32},{64,48},{80,64},{96,80},{112,96},{0,112},{1... | collective-permute-start | bytes 12296 | tf_op jit(solution)/shard_map/ppermute | solution.py:22
  42.2 55.6 %collective-permute-start.6 = (bf16[10,1,512]{2,0,1:T(8,128)(2,1)}, bf16[10,1,512]{2,0,1:T(8,128)(2,1)}, u32[]{:S(2)}, u32[]{:S(2)}) collective-permute-start(bf16[10,1,512]{2,0,1:T(8,128)(2,1)} %get-tuple-element.10), channel_id=1, source_target_pairs={{0,1},{1,2},{2,3},{3,4},{4,5},{5,6},{6,7},{7,8},{8,9},{9,10},{10,1... | collective-permute-start | bytes 30728 | tf_op jit(solution)/shard_map/ppermute | solution.py:21
  42.2 55.6 %collective-permute-start.7 = (bf16[10,1,512]{2,0,1:T(8,128)(2,1)}, bf16[10,1,512]{2,0,1:T(8,128)(2,1)}, u32[]{:S(2)}, u32[]{:S(2)}) collective-permute-start(bf16[10,1,512]{2,0,1:T(8,128)(2,1)} %get-tuple-element.11), channel_id=1, source_target_pairs={{1,0},{2,1},{3,2},{4,3},{5,4},{6,5},{7,6},{8,7},{9,8},{10,9},{11,1... | collective-permute-start | bytes 30728 | tf_op jit(solution)/shard_map/ppermute | solution.py:22
  51.9 61.2 %collective-permute-start.2 = (bf16[38,3,512]{2,1,0:T(4,128)(2,1)}, bf16[38,3,512]{2,1,0:T(4,128)(2,1)}, u32[]{:S(2)}, u32[]{:S(2)}) collective-permute-start(bf16[38,3,512]{2,1,0:T(4,128)(2,1)} %get-tuple-element.6), channel_id=1, source_target_pairs={{0,1},{1,2},{2,3},{3,4},{4,5},{5,6},{6,7},{7,8},{8,9},{9,10},{10,1... | collective-permute-start | bytes 350216 | tf_op jit(solution)/shard_map/ppermute | solution.py:21
  51.9 61.2 %collective-permute-start.3 = (bf16[38,3,512]{2,1,0:T(4,128)(2,1)}, bf16[38,3,512]{2,1,0:T(4,128)(2,1)}, u32[]{:S(2)}, u32[]{:S(2)}) collective-permute-start(bf16[38,3,512]{2,1,0:T(4,128)(2,1)} %get-tuple-element.7), channel_id=1, source_target_pairs={{1,0},{2,1},{3,2},{4,3},{5,4},{6,5},{7,6},{8,7},{9,8},{10,9},{11,1... | collective-permute-start | bytes 350216 | tf_op jit(solution)/shard_map/ppermute | solution.py:22
  57.2 4.4 %copy-start.4 = (bf16[1,512,1536]{2,1,0:T(8,128)(2,1)S(1)}, bf16[1,512,1536]{2,1,0:T(8,128)(2,1)}, u32[]{:S(2)}) copy-start(bf16[1,512,1536]{2,1,0:T(8,128)(2,1)} %param.35) | copy-start | bytes 4718596
  65.7 6.7 %copy-start.30 = (pred[6,256]{1,0:T(8,128)(4,1)S(1)}, pred[6,256]{1,0:T(8,128)(4,1)}, u32[]{:S(2)}) copy-start(pred[6,256]{1,0:T(8,128)(4,1)} %compare_and_fusion.1) | copy-start | bytes 4612
  72.4 7.3 %copy-start.14 = (bf16[1,1536,512]{2,1,0:T(8,128)(2,1)S(1)}, bf16[1,1536,512]{2,1,0:T(8,128)(2,1)}, u32[]{:S(2)}) copy-start(bf16[1,1536,512]{2,1,0:T(8,128)(2,1)} %param.37) | copy-start | bytes 4718596
  85.1 5.6 %copy-start.7 = (bf16[1536,512]{1,0:T(8,128)(2,1)}, bf16[1536,512]{1,0:T(8,128)(2,1)S(1)}, u32[]{:S(2)}) copy-start(bf16[1536,512]{1,0:T(8,128)(2,1)S(1)} %fusion.2) | copy-start | bytes 4718596
  86.3 5.7 %copy-start.26 = (f32[1,512]{1,0:T(1,128)S(1)}, f32[1,512]{1,0:T(1,128)}, u32[]{:S(2)}) copy-start(f32[1,512]{1,0:T(1,128)} %param.45) | copy-start | bytes 6148
  86.3 5.7 %copy-start.27 = (f32[1,512]{1,0:T(1,128)S(1)}, f32[1,512]{1,0:T(1,128)}, u32[]{:S(2)}) copy-start(f32[1,512]{1,0:T(1,128)} %param.44) | copy-start | bytes 6148
  95.9 5.3 %copy-start.2 = (bf16[1,512,1536]{2,1,0:T(8,128)(2,1)S(1)}, bf16[1,512,1536]{2,1,0:T(8,128)(2,1)}, u32[]{:S(2)}) copy-start(bf16[1,512,1536]{2,1,0:T(8,128)(2,1)} %param.40) | copy-start | bytes 4718596
  113.0 4.9 %copy-start.6 = (bf16[1,512,1536]{2,1,0:T(8,128)(2,1)S(1)}, bf16[1,512,1536]{2,1,0:T(8,128)(2,1)}, u32[]{:S(2)}) copy-start(bf16[1,512,1536]{2,1,0:T(8,128)(2,1)} %param.34) | copy-start | bytes 4718596
  122.9 23.2 %copy-start.29 = (pred[6,512]{1,0:T(8,128)(4,1)S(1)}, pred[6,512]{1,0:T(8,128)(4,1)}, u32[]{:S(2)}) copy-start(pred[6,512]{1,0:T(8,128)(4,1)} %compare_and_fusion) | copy-start | bytes 9220
  146.1 14.8 %copy-start.16 = (bf16[1,1536,512]{2,1,0:T(8,128)(2,1)S(1)}, bf16[1,1536,512]{2,1,0:T(8,128)(2,1)}, u32[]{:S(2)}) copy-start(bf16[1,1536,512]{2,1,0:T(8,128)(2,1)} %param.37) | copy-start | bytes 4718596
  177.5 5.4 %copy-start.9 = (bf16[32,16,512]{2,1,0:T(8,128)(2,1)S(1)}, bf16[32,16,512]{2,1,0:T(8,128)(2,1)}, u32[]{:S(2)}) copy-start(bf16[32,16,512]{2,1,0:T(8,128)(2,1)} %param.24) | copy-start | bytes 1572868
  (20 other events, 43.8 us)
